TPU v7x, 32 devices: a whole 2x2x4 slice. The times are simulated.
32 devices in a mesh: row: 4 (over z_hi, core), col: 4 (over y, x), depth: 2 (over z_lo).
Axes of the slice: x: 2, y: 2, z: 4 (z_hi: 2, z_lo: 2; z = z_hi * 2 + z_lo), core: 2. Of those that a mesh axis runs over, the one named last changes fastest.
Arguments:
- matrix: bfloat16 [20480, 20480], P(('col', 'depth'), 'row'), may hold values from 0 to 250, as said below
- swaps: int32 [512], replicated, may hold values from 512 to 20479, as said below
- inverse_first: bfloat16 [256, 256], replicated, may hold values from 0 to 250, as said below
- inverse_second: bfloat16 [256, 256], replicated, may hold values from 0 to 250, as said below
Outputs:
- updated: bfloat16 [20480, 20480], P(('col', 'depth'), 'row')
Inputs may be any that keep to these rules, and one draw needn't show every extreme that they name: `matrix`: whole numbers. Whole numbers; inverse_first times the block of permuted at rows and columns 0 to 255 is the identity modulo 251. Whole numbers; inverse_second times the block of first_update at rows and columns 256 to 511 is the identity modulo 251. `swaps`: distinct rows, none below 512.
All inputs are finite; a program needn't handle non-finite values.
Results may differ from a plain program's by a relative error of at most 0.001.
Values may be sent and summed in bfloat16 or wider, within the bound.
No kernel may reach another device: no remote copies, remote signals or barrier semaphores. Data moves between devices by JAX's collectives and lax.ppermute only.
A program may use at most 320 MiB of HBM per device.

v0:
```python
import jax
import jax.numpy as jnp
from jax import lax
from jax.sharding import PartitionSpec as P

centre = 125.0


def from_root(value, axis, source):
    kept = jnp.where(lax.axis_index(axis) == source, value, 0).astype(value.dtype)
    return lax.psum(kept, axis)


def residue(values):
    return jnp.mod(values, 251.0)


def split_inner(multipliers):
    return lax.all_to_all(multipliers, "depth", split_axis=1, concat_axis=0, tiled=True)


def local(matrix, swaps, inverse_first, inverse_second):
    local_rows = matrix.shape[0]
    block_cols = matrix.shape[1]
    panel_width = inverse_first.shape[0]
    pair_count = swaps.shape[0]
    depth_count = lax.axis_size("depth")
    first_row = (lax.axis_index("col") * depth_count + lax.axis_index("depth")) * local_rows
    first_col = lax.axis_index("row") * block_cols
    pair_index = jnp.arange(pair_count, dtype=jnp.int32)
    sources = jnp.concatenate([swaps, pair_index]) - first_row
    owned_mask = (sources >= 0) & (sources < local_rows)
    picked = jnp.take(matrix, jnp.clip(sources, 0, local_rows - 1), axis=0)
    picked = jnp.where(owned_mask[:, None], picked, jnp.zeros_like(picked))
    moved_rows = lax.psum(picked, ("col", "depth")).astype(jnp.float32).astype(jnp.bfloat16)
    pivot_rows = moved_rows[:pair_count]
    destinations = jnp.concatenate([pair_index, swaps]) - first_row
    valid_mask = (destinations >= 0) & (destinations < local_rows)
    destinations = jnp.where(valid_mask, destinations, local_rows)
    permuted = matrix.at[destinations].set(
        jnp.concatenate([pivot_rows, moved_rows[pair_count:]], axis=0), mode="drop"
    )
    row_index = first_row + jnp.arange(local_rows, dtype=jnp.int32)
    head_index = first_col + jnp.arange(pair_count, dtype=jnp.int32)
    u_first = pivot_rows[:panel_width]
    l_top = residue(
        jnp.dot(
            pivot_rows[panel_width:, :panel_width],
            inverse_first,
            preferred_element_type=jnp.float32,
        )
    ).astype(jnp.bfloat16)
    l_first = residue(
        jnp.dot(permuted[:, :panel_width], inverse_first, preferred_element_type=jnp.float32)
    )
    l_first = jnp.where(row_index[:, None] >= panel_width, l_first, jnp.zeros_like(l_first)).astype(
        jnp.bfloat16
    )
    l_first, l_top = (from_root(l_first, "row", 0), from_root(l_top, "row", 0))
    u_second = residue(
        pivot_rows[panel_width:].astype(jnp.float32)
        - jnp.dot(l_top, u_first, preferred_element_type=jnp.float32)
    ).astype(jnp.bfloat16)
    half_width = panel_width // depth_count
    depth_start = lax.axis_index("depth") * half_width
    group_first = split_inner(l_first)
    first_half = lax.dynamic_slice_in_dim(u_first, depth_start, half_width, 0)
    second_half = lax.dynamic_slice_in_dim(u_second, depth_start, half_width, 0)
    panel_term = (
        residue(
            jnp.dot(
                group_first,
                first_half[:, panel_width:pair_count],
                preferred_element_type=jnp.float32,
            )
        )
        - centre
    )
    panel_total = lax.psum_scatter(
        panel_term.astype(jnp.bfloat16), "depth", scatter_dimension=0, tiled=True
    ).astype(jnp.float32)
    panel_cols = residue(
        permuted[:, panel_width:pair_count].astype(jnp.float32) - panel_total - centre * depth_count
    )
    l_second = residue(
        jnp.dot(panel_cols.astype(jnp.bfloat16), inverse_second, preferred_element_type=jnp.float32)
    )
    l_second = jnp.where(
        row_index[:, None] >= pair_count, l_second, jnp.zeros_like(l_second)
    ).astype(jnp.bfloat16)
    l_second = from_root(l_second, "row", 0)
    group_second = split_inner(l_second)
    summed = jnp.dot(group_first, first_half, preferred_element_type=jnp.float32) + jnp.dot(
        group_second, second_half, preferred_element_type=jnp.float32
    )
    block_total = lax.psum_scatter(
        (residue(summed) - centre).astype(jnp.bfloat16), "depth", scatter_dimension=0, tiled=True
    ).astype(jnp.float32)
    final_update = residue(permuted.astype(jnp.float32) - block_total - centre * depth_count)
    multipliers = jnp.concatenate([l_first, l_second], axis=1).astype(jnp.float32)
    store_mask = (head_index[None, :] < panel_width) & (row_index[:, None] >= panel_width) | (
        head_index[None, :] >= panel_width
    ) & (head_index[None, :] < pair_count) & (row_index[:, None] >= pair_count)
    head_part = jnp.where(store_mask, multipliers, final_update[:, :pair_count])
    stored = jnp.concatenate([head_part, final_update[:, pair_count:]], axis=1)
    return (stored * (1.0 / 251.0)).astype(jnp.bfloat16)


def solution(mesh):
    return jax.shard_map(
        local,
        mesh=mesh,
        in_specs=(P(("col", "depth"), "row"), P(), P(), P()),
        out_specs=P(("col", "depth"), "row"),
        check_vma=False,
    )
```

profile of v0, /device:TPU:26, one launch (start us, length us, event | category | flops | bytes accessed | tf_op | source)
XLA Modules:
  0.0 1568.7 jit_solution(10889153300699355335)
XLA Ops:
  6.5 0.0 copy-start
  6.5 0.0 all-reduce.6.cloned.1.call-start
  6.5 18.3 %copy.19 = bf16[2560,5120]{1,0:T(8,128)(2,1)} copy(bf16[2560,5120]{1,0:T(8,128)(2,1)} %param.4) | data formatting | bytes 52428800
  24.9 0.0 copy-done.9
  25.0 30.4 %gather_fusion = bf16[1024,5120]{1,0:T(8,128)(2,1)} fusion(bf16[2560,5120]{1,0:T(8,128)(2,1)} %copy.19, s32[1024]{0:T(1024)S(1)} %broadcast_clamp_fusion.1), kind=kCustom, calls=%fused_computation | custom fusion | bytes 20975616 | tf_op jit(solution)/shard_map/jit(_take)/gather | solution.py:33
  55.3 10.5 select_select_fusion
  65.8 0.0 all-reduce.6.cloned.1.call-update
  65.8 0.0 all-reduce.8.cloned.1.call-start
  65.9 3.8 sort
  69.7 0.0 copy-start.5
  69.7 409.5 %all-reduce.6.cloned.1.call-done = bf16[1024,5120]{1,0:T(8,128)(2,1)} async-done(((bf16[1024,5120]{1,0:T(8,128)(2,1)}), bf16[1024,5120]{1,0:T(8,128)(2,1)}) %all-reduce.6.cloned.1.call-update) | async-done | bytes 10485776 | tf_op jit(solution)/shard_map/psum | solution.py:35
  479.3 89.4 %scatter_custom_fusion = bf16[2560,5120]{1,0:T(8,128)(2,1)} fusion(bf16[2560,5120]{1,0:T(8,128)(2,1)} %copy.19, s32[1024]{0:T(1024)S(1)} %get-tuple-element.5, bf16[1024,5120]{1,0:T(8,128)(2,1)} %all-reduce.6.cloned.1.call-done, s32[1024]{0:T(1024)S(1)} %broadcast_clamp_fusion), kind=kCustom, calls=%fused_computation.11 | custom fusion | bytes 26214400 | tf_op jit(solution)/shard_map/scatter | solution.py:40
  568.6 0.0 copy-done.5
  568.6 0.0 copy-done
  568.6 4.2 fusion.18
  572.9 0.0 all-reduce.8.cloned.1.call-update
  572.9 59.1 %all-reduce.8.cloned.1.call-done = bf16[2560,256]{1,0:T(8,128)(2,1)} async-done(((bf16[2560,256]{1,0:T(8,128)(2,1)}), bf16[2560,256]{1,0:T(8,128)(2,1)}) %all-reduce.8.cloned.1.call-update) | async-done | bytes 1310736 | tf_op jit(solution)/shard_map/psum | solution.py:11
  632.0 2.6 copy_bitcast_fusion.1
  634.6 4.5 all-to-all-start
  639.1 0.0 reduce-scatter.6.cloned.1.call-start
  639.2 5.6 slice_convert_fusion
  644.8 9.2 all-to-all-done
  654.0 5.3 fusion.9
  659.3 0.0 reduce-scatter.6.cloned.1.call-update
  659.3 0.0 all-reduce.10.cloned.1.call-start
  659.4 0.0 copy-start.7
  659.4 1.9 fusion.31
  661.2 36.9 %reduce-scatter.6.cloned.1.call-done = bf16[2560,256]{1,0:T(8,128)(2,1)} async-done(((bf16[5120,256]{1,0:T(8,128)(2,1)}), bf16[2560,256]{1,0:T(8,128)(2,1)}) %reduce-scatter.6.cloned.1.call-update) | async-done | bytes 1310736 | tf_op jit(solution)/shard_map/reduce_scatter | solution.py:79
  698.1 0.0 copy-done.10
  698.1 5.5 fusion.17
  703.6 0.0 copy-done.7
  703.6 0.0 all-reduce.10.cloned.1.call-update
  703.6 64.3 %all-reduce.10.cloned.1.call-done = (bf16[2560,256]{1,0:T(8,128)(2,1)}, bf16[256,256]{1,0:T(8,128)(2,1)}) async-done(((bf16[2560,256]{1,0:T(8,128)(2,1)}, bf16[256,256]{1,0:T(8,128)(2,1)}), (bf16[2560,256]{1,0:T(8,128)(2,1)}, bf16[256,256]{1,0:T(8,128)(2,1)})) %all-reduce.10.cloned.1.call-update) | async-done | bytes 1441808 | tf_op jit(solution)/shard_map/psum | solution.py:11
  768.0 2.6 copy_bitcast_fusion
  770.5 4.5 all-to-all-start.1
  775.1 0.0 copy-start.4
  775.1 0.0 reduce-scatter.8.cloned.1.call-start
  775.1 37.4 %fusion.26 = f32[5120,5120]{1,0:T(8,128)} fusion(bf16[5120,128]{1,0:T(8,128)(2,1)} %bitcast.4, bf16[256,5120]{1,0:T(8,128)(2,1)S(1)} %get-tuple-element.10, s32[]{:T(128)S(6)} %select_n.120), kind=kOutput, calls=%fused_computation.44 | convolution fusion | flops 6710886400 | bytes 107479040 | tf_op jit(solution)/shard_map/dot_general | solution.py:93
  812.5 4.9 fusion.48
  817.4 0.0 all-to-all-done.1
  817.4 71.7 %fusion.2 = bf16[5120,5120]{1,0:T(8,128)(2,1)} fusion(f32[5120,5120]{1,0:T(8,128)} %fusion.26, bf16[5120,128]{1,0:T(8,128)(2,1)} %bitcast.7, f32[256,5120]{1,0:T(8,128)} %fusion.48, s32[]{:T(128)S(6)} %select_n.120, f32[256,5120]{1,0:T(8,128)} %get-tuple-element.9), kind=kOutput, calls=%fused_computation.5 | convolution fusion | flops 6952058880 | bytes 163840000 | tf_op jit(solution)/shard_map/dot_general | solution.py:93
  889.1 0.0 reduce-scatter.8.cloned.1.call-update
  889.1 571.7 %reduce-scatter.8.cloned.1.call-done = bf16[2560,5120]{1,0:T(8,128)(2,1)} async-done(((bf16[5120,5120]{1,0:T(8,128)(2,1)}), bf16[2560,5120]{1,0:T(8,128)(2,1)}) %reduce-scatter.8.cloned.1.call-update) | async-done | bytes 26214416
  1460.9 35.6 %add_select_fusion.1 = f32[2560,5120]{1,0:T(8,128)} fusion(bf16[2560,5120]{1,0:T(8,128)(2,1)} %reduce-scatter.8.cloned.1.call-done, bf16[2560,5120]{1,0:T(8,128)(2,1)} %scatter_custom_fusion), kind=kLoop, calls=%fused_computation.7 | loop fusion | flops 131072000 | bytes 104857600 | tf_op jit(solution)/shard_map/jit(remainder)/select_n | solution.py:15
  1496.5 32.9 %slice.48 = f32[2560,4608]{1,0:T(8,128)} slice(f32[2560,5120]{1,0:T(8,128)} %add_select_fusion.1), slice={[0:2560], [512:5120]} | slice | bytes 94371840 | tf_op jit(solution)/shard_map/slice | solution.py:105
  1529.4 0.0 copy-done.6
  1529.4 6.0 slice_select_fusion
  1535.5 26.5 %fusion.3 = bf16[2560,5120]{1,0:T(8,128)(2,1)} fusion(f32[2560,4608]{1,0:T(8,128)} %slice.48, f32[2560,512]{1,0:T(8,128)} %slice_select_fusion), kind=kLoop, calls=%fused_computation.9 | loop fusion | flops 39321600 | bytes 78643200 | tf_op jit(solution)/shard_map/convert_element_type | solution.py:106
  (23 shorter events, 0.1 us)
Async XLA Ops:
  6.5 562.1 %copy-start = (bf16[256,256]{1,0:T(8,128)(2,1)S(1)}, bf16[256,256]{1,0:T(8,128)(2,1)}, u32[]{:S(2)}) copy-start(bf16[256,256]{1,0:T(8,128)(2,1)} %param.6) | copy-start | bytes 393220
  6.5 18.3 %copy-start.9 = (s32[512]{0:T(512)S(1)}, s32[512]{0:T(512)}, u32[]{:S(2)}) copy-start(s32[512]{0:T(512)} %param.5) | copy-start | bytes 6148
  6.5 472.7 %all-reduce.6.cloned.1.call-start = ((), (), s32[]{:S(2)}) async-start(), calls=%async_computation.4 | async-start | bytes 20971520 | tf_op jit(solution)/shard_map/psum | solution.py:35
  65.8 566.1 %all-reduce.8.cloned.1.call-start = ((), (), s32[]{:S(2)}) async-start(), calls=%async_computation.5 | async-start | bytes 2621440 | tf_op jit(solution)/shard_map/psum | solution.py:11
  69.7 498.9 %copy-start.5 = (pred[2560]{0:T(1024)(128)(4,1)}, pred[2560]{0:T(1024)(128)(4,1)S(1)}, u32[]{:S(2)}) copy-start(pred[2560]{0:T(1024)(128)(4,1)S(1)} %fusion.35) | copy-start | bytes 7684
  634.6 19.4 %all-to-all-start = ((bf16[2560,2,128]{2,0,1:T(8,128)(2,1)}), bf16[2560,2,128]{2,0,1:T(8,128)(2,1)}, u32[]{:S(2)}, u32[]{:S(2)}) async-start(bf16[2560,2,128]{2,0,1:T(8,128)(2,1)} %copy_bitcast_fusion.1), calls=%async_computation | async-start | bytes 2621440 | tf_op jit(solution)/shard_map/all_to_all | solution.py:19
  639.1 59.0 %reduce-scatter.6.cloned.1.call-start = ((), (), s32[]{:S(2)}) async-start(), calls=%async_computation.6 | async-start | bytes 3932160 | tf_op jit(solution)/shard_map/reduce_scatter | solution.py:79
  654.0 44.1 %copy-start.10 = (bf16[256,256]{1,0:T(8,128)(2,1)S(1)}, bf16[256,256]{1,0:T(8,128)(2,1)}, u32[]{:S(2)}) copy-start(bf16[256,256]{1,0:T(8,128)(2,1)} %param.7) | copy-start | bytes 393220
  659.3 108.7 %all-reduce.10.cloned.1.call-start = ((), (), s32[]{:S(2)}) async-start(), calls=%async_computation.8 | async-start | bytes 2883584 | tf_op jit(solution)/shard_map/psum | solution.py:11
  659.4 44.3 %copy-start.7 = (pred[2560]{0:T(1024)(128)(4,1)}, pred[2560]{0:T(1024)(128)(4,1)S(1)}, u32[]{:S(2)}) copy-start(pred[2560]{0:T(1024)(128)(4,1)S(1)} %fusion.34) | copy-start | bytes 7684
  770.5 46.9 %all-to-all-start.1 = ((bf16[2560,2,128]{2,0,1:T(8,128)(2,1)}), bf16[2560,2,128]{2,0,1:T(8,128)(2,1)}, u32[]{:S(2)}, u32[]{:S(2)}) async-start(bf16[2560,2,128]{2,0,1:T(8,128)(2,1)} %copy_bitcast_fusion), calls=%async_computation.2 | async-start | bytes 2621440 | tf_op jit(solution)/shard_map/all_to_all | solution.py:19
  775.1 37.5 %copy-start.4 = (bf16[256,256]{1,0:T(8,128)(2,1)S(1)}, bf16[256,256]{1,0:T(8,128)(2,1)}, u32[]{:S(2)}) copy-start(bf16[256,256]{1,0:T(8,128)(2,1)} %get-tuple-element.8) | copy-start | bytes 393220
  775.1 685.8 %reduce-scatter.8.cloned.1.call-start = ((), (), s32[]{:S(2)}) async-start(), calls=%async_computation.7 | async-start | bytes 78643200
  1496.4 33.0 %copy-start.2 = (bf16[2560,256]{1,0:T(8,128)(2,1)S(1)}, bf16[2560,256]{1,0:T(8,128)(2,1)}, u32[]{:S(2)}) copy-start(bf16[2560,256]{1,0:T(8,128)(2,1)} %all-reduce.8.cloned.1.call-done) | copy-start | bytes 3932164
  1496.5 33.0 %copy-start.3 = (bf16[2560,256]{1,0:T(8,128)(2,1)S(1)}, bf16[2560,256]{1,0:T(8,128)(2,1)}, u32[]{:S(2)}) copy-start(bf16[2560,256]{1,0:T(8,128)(2,1)} %get-tuple-element.7) | copy-start | bytes 3932164
  1496.5 33.0 %copy-start.6 = (pred[2560]{0:T(1024)(128)(4,1)S(1)}, pred[2560]{0:T(1024)(128)(4,1)}, u32[]{:S(2)}) copy-start(pred[2560]{0:T(1024)(128)(4,1)} %copy-done.5) | copy-start | bytes 7684
  1496.5 33.0 %copy-start.8 = (pred[2560]{0:T(1024)(128)(4,1)S(1)}, pred[2560]{0:T(1024)(128)(4,1)}, u32[]{:S(2)}) copy-start(pred[2560]{0:T(1024)(128)(4,1)} %copy-done.7) | copy-start | bytes 7684
  1535.5 26.5 %copy-start.1 = (bf16[256,256]{1,0:T(8,128)(2,1)S(1)}, bf16[256,256]{1,0:T(8,128)(2,1)}, u32[]{:S(2)}) copy-start(bf16[256,256]{1,0:T(8,128)(2,1)} %param.6) | copy-start | bytes 393220
Sparse Core Ops, SparseCore 0:
  66.0 413.2 all-reduce.5
  573.0 58.8 all-reduce.7
  659.4 38.6 reduce-scatter.5
  703.8 64.1 all-reduce.9
  889.2 571.5 reduce-scatter.7
where the time goes:
time: 1570 us
  waiting for transfers between devices  1150 us (73%)
  local copies, waits for them, and re-layouts  176 us (11%)
  matrix products  131 us (8%)
  other arithmetic  88.1 us (6%)
    unnamed x6, waiting for transfers between devices  572 us
    psum x1, waiting for transfers between devices, local(): lax.psum(picked, ('col', 'depth')).astype(jnp.float32).astype(jnp.bfloat16)  410 us
    psum x2, waiting for transfers between devices, from_root(): return lax.psum(kept, axis)  123 us
    scatter x2, local copies, waits for them, and re-layouts, local(): matrix.at[destinations]  89.4 us
    dot_general x1, matrix products, local(): jnp.dot(group_second, second_half, preferred_element_type=jnp.float32)  71.7 us
    dot_general x1, matrix products, local(): jnp.dot(group_first, first_half, preferred_element_type=jnp.float32)  37.4 us
    reduce_scatter x1, waiting for transfers between devices, local(): lax.psum_scatter(panel_term.astype(jnp.bfloat16), 'depth', scatter_dimens...  36.9 us
    select_n x1, other arithmetic, residue(): return jnp.mod(values, 251.0)  35.6 us
  transfers between devices with their start and end apart: 7, of which 6 were waited for; matrix products, arithmetic and copies ran while one was open for 3% of the time, Pallas kernels for 0%

commit v1 on v0

v1 whole, which is shorter than its diff:
```python
import functools

import jax
import jax.numpy as jnp
from jax import lax
from jax.experimental import pallas as pl
from jax.experimental.pallas import tpu as pltpu
from jax.sharding import PartitionSpec as P

modulus = 251.0
scale = 1.0 / 251.0
blocks_axes = ("col", "depth")
f32 = jnp.float32
bf16 = jnp.bfloat16


def dot(a, b):
    return jnp.dot(a, b, preferred_element_type=f32)


def centred(values):
    return values - modulus * jnp.round(values * scale)


def centred_bf16(values):
    return jnp.where(values > 125, values - 251, values).astype(bf16)


def lifted(values):
    return jnp.where(values < 0, values + modulus, values)


def floor_residue(values):
    return values - modulus * jnp.floor((values + 0.5) * scale)


def split_columns(total, parts):
    tiles = total // 128
    edges = [128 * (tiles * k // parts) for k in range(parts + 1)]
    return list(zip(edges[:-1], edges[1:]))


def panel_weights(a, inverse_first, inverse_second, upper, l_top, keep_first, keep_second):
    l_first = centred(dot(a[:, :256], inverse_first))
    if keep_first is not None:
        l_first = jnp.where(keep_first, l_first, 0.0)
    first = l_first.astype(bf16)
    rest = centred(a[:, 256:].astype(f32) - dot(first, upper))
    l_second = centred(dot(rest.astype(bf16), inverse_second))
    if keep_second is not None:
        l_second = jnp.where(keep_second, l_second, 0.0)
    second = l_second.astype(bf16)
    weight_first = centred(l_first - dot(second, l_top)).astype(bf16)
    return l_first, l_second, jnp.concatenate([weight_first, second], axis=1)


def place_kernel(count, spans, step, onehot_ref, *refs):
    parts, out_ref = refs[:-1], refs[-1]
    onehot = onehot_ref[...]
    for t, (lo, hi) in enumerate(spans):
        for c in range(lo, hi, step):
            w = min(step, hi - c)
            stacked = jnp.concatenate(
                [parts[t * count + k][:, c - lo : c - lo + w] for k in range(count)], axis=0
            )
            out_ref[:, c : c + w] = dot(onehot, stacked).astype(bf16)


def place(onehot, parts, spans, count):
    width = spans[-1][1]
    return pl.pallas_call(
        functools.partial(place_kernel, count, spans, 512),
        out_shape=jax.ShapeDtypeStruct((onehot.shape[0], width), bf16),
        compiler_params=pltpu.CompilerParams(vmem_limit_bytes=40 << 20),
        name="place",
    )(onehot, *parts)


def update_kernel(
    base_row, tile, step, has_alias, info, a_ref, m_ref, p_ref, pb_ref, if_ref, is_ref, up_ref, lt_ref, *rest
):
    out_ref = rest[-1]
    tile_row = base_row + pl.program_id(0) * tile
    global_row = info[0] + tile_row
    rows = global_row + lax.broadcasted_iota(jnp.int32, (tile, 1), 0)
    pivots = p_ref.shape[0]
    a = a_ref[...]
    top = base_row < pivots
    in_pivots = (info[0] == 0) & (tile_row < pivots)
    if top:
        start = pl.multiple_of(jnp.minimum(tile_row, pivots - tile), tile)
        window = pl.ds(start, tile)
        a = jnp.where(in_pivots, pb_ref[window, :], a)
    l_first, l_second, weights = panel_weights(
        a, if_ref[...], is_ref[...], up_ref[...], lt_ref[...], rows >= 256, rows >= 512
    )
    width = m_ref.shape[1]
    for c in range(0, width, step):
        m = m_ref[:, c : c + step]
        if top:
            m = jnp.where(in_pivots, p_ref[window, c : c + step], m)
        value = m.astype(f32) - dot(weights, p_ref[:, c : c + step])
        out_ref[:, c : c + step] = (floor_residue(value) * scale).astype(bf16)

    @pl.when(info[1] == 0)
    def _():
        old = out_ref[:, :256]
        out_ref[:, :256] = jnp.where(rows >= 256, (lifted(l_first) * scale).astype(bf16), old)
        old = out_ref[:, 256:512]
        out_ref[:, 256:512] = jnp.where(rows >= 512, (lifted(l_second) * scale).astype(bf16), old)


def update(info, base_row, rows, tile, a, matrix, pivots, small, out):
    height, width = matrix.shape
    step = 512 if width % 512 == 0 else 256
    base = base_row // tile
    whole = lambda x: pl.BlockSpec(x.shape, lambda i, s: (0, 0), pipeline_mode=pl.Buffered(1))
    in_specs = [
        pl.BlockSpec((tile, a.shape[1]), lambda i, s: (i, 0)),
        pl.BlockSpec((tile, width), lambda i, s: (base + i, 0)),
        whole(pivots),
    ] + [whole(x) for x in small]
    operands = [a, matrix, pivots, *small]
    aliases = {}
    if out is not None:
        in_specs.append(pl.BlockSpec(memory_space=pl.ANY))
        operands.append(out)
        aliases = {len(operands): 0}
    return pl.pallas_call(
        functools.partial(update_kernel, base_row, tile, step, out is not None),
        out_shape=jax.ShapeDtypeStruct((height, width), bf16),
        grid_spec=pltpu.PrefetchScalarGridSpec(
            num_scalar_prefetch=1,
            grid=(rows // tile,),
            in_specs=in_specs,
            out_specs=pl.BlockSpec((tile, width), lambda i, s: (base + i, 0)),
        ),
        input_output_aliases=aliases,
        compiler_params=pltpu.CompilerParams(vmem_limit_bytes=48 << 20),
        cost_estimate=pl.CostEstimate(
            flops=2 * rows * 512 * width, bytes_accessed=4 * rows * width, transcendentals=0
        ),
        name="update",
    )(info, *operands)


def merge_kernel(
    spans, info, groups, spread_ref, mask_ref, p_ref, if_ref, is_ref, up_ref, lt_ref, *rest
):
    q_refs = rest[: len(spans)]
    out_in, out_ref, held, fresh, sem_in, sem_out = rest[len(spans) :]
    count = info[2]
    width = p_ref.shape[1]

    def fetch(u):
        source = out_ref.at[pl.ds(pl.multiple_of(groups[u] * 8, 8), 8), :]
        return pltpu.make_async_copy(source, held.at[u], sem_in.at[u])

    def write(u):
        target = out_ref.at[pl.ds(pl.multiple_of(groups[u] * 8, 8), 8), :]
        return pltpu.make_async_copy(held.at[u], target, sem_out.at[u])

    @pl.loop(0, count)
    def _(u):
        fetch(u).start()

    lo, hi = spans[-1]
    a = q_refs[-1][:, width - lo : hi - lo]
    l_first, l_second, weights = panel_weights(
        a, if_ref[...], is_ref[...], up_ref[...], lt_ref[...], None, None
    )
    for k, (lo, hi) in enumerate(spans):
        top = min(hi, width)
        for c in range(lo, top, 512):
            w = min(512, top - c)
            value = q_refs[k][:, c - lo : c - lo + w].astype(f32) - dot(weights, p_ref[:, c : c + w])
            fresh[:, c : c + w] = (floor_residue(value) * scale).astype(bf16)

    @pl.when(info[1] == 0)
    def _():
        fresh[:, :256] = (lifted(l_first) * scale).astype(bf16)
        fresh[:, 256:512] = (lifted(l_second) * scale).astype(bf16)

    @pl.loop(0, count)
    def _(u):
        fetch(u).wait()

    slots = held.shape[0]
    for c in range(0, width, 256):
        spread = dot(spread_ref[...], fresh[:, c : c + 256]).astype(bf16)
        old = held[:, :, c : c + 256].reshape(slots * 8, 256)
        new = jnp.where(mask_ref[...] > 0, spread, old)
        held[:, :, c : c + 256] = new.reshape(slots, 8, 256)

    @pl.loop(0, count)
    def _(u):
        write(u).start()

    @pl.loop(0, count)
    def _(u):
        write(u).wait()


def merge(info, groups, spread, mask, pivots, small, parts, spans, out):
    slots = groups.shape[0]
    width = out.shape[1]
    vmem = pl.BlockSpec(memory_space=pltpu.VMEM)
    anywhere = pl.BlockSpec(memory_space=pl.ANY)
    operands = [spread, mask, pivots, *small, *parts, out]
    return pl.pallas_call(
        functools.partial(merge_kernel, spans),
        out_shape=jax.ShapeDtypeStruct(out.shape, bf16),
        grid_spec=pltpu.PrefetchScalarGridSpec(
            num_scalar_prefetch=2,
            grid=(1,),
            in_specs=[vmem] * (len(operands) - 1) + [anywhere],
            out_specs=anywhere,
            scratch_shapes=[
                pltpu.VMEM((slots, 8, width), bf16),
                pltpu.VMEM((slots, width), bf16),
                pltpu.SemaphoreType.DMA((slots,)),
                pltpu.SemaphoreType.DMA((slots,)),
            ],
        ),
        input_output_aliases={len(operands) + 1: 0},
        compiler_params=pltpu.CompilerParams(vmem_limit_bytes=56 << 20),
        cost_estimate=pl.CostEstimate(
            flops=4 * slots * 512 * width, bytes_accessed=32 * slots * width, transcendentals=0
        ),
        name="merge",
    )(info, groups, *operands)


def local(matrix, swaps, inverse_first, inverse_second):
    height, width = matrix.shape
    panel = inverse_first.shape[0]
    pivots = swaps.shape[0]
    col_count, depth_count, row_count = (
        lax.axis_size("col"), lax.axis_size("depth"), lax.axis_size("row"))
    count = col_count * depth_count
    levels = count.bit_length() - 1
    me = lax.axis_index("col") * depth_count + lax.axis_index("depth")
    row = lax.axis_index("row")
    first_row = me * height
    mean = pivots // count
    slots = -(-(mean + 4 * int(mean**0.5)) // 32) * 32

    def hop(value, bit):
        return lax.ppermute(value, blocks_axes, [(i, i ^ (1 << bit)) for i in range(count)])

    def along_row(value):
        reach = row_count // 2
        while reach:
            pairs = [(i, i + reach) for i in range(0, row_count, 2 * reach)]
            got = lax.ppermute(value, "row", pairs)
            value = jnp.where(row % (2 * reach) == reach, got, value)
            reach //= 2
        return value

    orders = [[(k + s) % levels for k in range(levels)] for s in range(0, levels, -(-levels // 3))]
    spans = split_columns(width, len(orders))
    wide_spans = split_columns(width + pivots, len(orders))

    owner = swaps // height
    index = jnp.arange(pivots, dtype=jnp.int32)
    earlier = (owner[:, None] == owner[None, :]) & (index[None, :] < index[:, None])
    rank = jnp.sum(earlier.astype(jnp.int32), axis=1)
    rounds = jnp.max(rank) // slots + 1
    slot_index = jnp.arange(slots, dtype=jnp.int32)
    all_slots = jnp.arange(count * slots, dtype=jnp.int32)

    def round_slots(turn):
        place_in = rank - turn * slots
        valid = (place_in >= 0) & (place_in < slots)
        mine = (valid & (owner == me))[None, :] & (place_in[None, :] == slot_index[:, None])
        rows = jnp.sum(jnp.where(mine, (swaps - first_row)[None, :], 0), axis=1)
        used = jnp.any(mine, axis=1)
        return place_in, valid, rows, used

    def pivot_exchange(turn):
        place_in, valid, rows, used = round_slots(turn)
        picked = jnp.take(matrix, rows, axis=0, mode="clip")
        picked = centred_bf16(jnp.where(used[:, None], picked, 0))
        key = jnp.where(valid, (owner ^ me) * slots + place_in, -1)
        onehot = (key[:, None] == all_slots[None, :]).astype(bf16)
        head = along_row(picked[:, :pivots])
        for bit in range(levels):
            head = jnp.concatenate([head, hop(head, bit)], axis=0)
        parts = []
        for order, (lo, hi) in zip(orders, spans):
            held = {0: picked[:, lo:hi]}
            for bit in order:
                held.update({mask | (1 << bit): hop(held[mask], bit) for mask in list(held)})
            parts += [held[mask] for mask in range(count)]
        return place(onehot, parts, spans, count), dot(onehot, head).astype(bf16)

    def swapped_out(turn, top_panel):
        place_in, valid, rows, used = round_slots(turn)
        parts = []
        for order, (lo, hi) in zip(orders, wide_spans):
            ordered = sum(((owner >> bit) & 1) << (levels - 1 - k) for k, bit in enumerate(order))
            key = jnp.where(valid, ordered * slots + place_in, -1)
            onehot = (all_slots[:, None] == key[None, :]).astype(bf16)
            source = matrix[:pivots, lo : min(hi, width)]
            if hi > width:
                source = jnp.concatenate([source, top_panel], axis=1)
            value = dot(onehot, source).astype(bf16)
            reached = [0]
            for bit in order:
                half = value.shape[0] // 2
                got = lax.ppermute(
                    value[half:], blocks_axes, [(i, i | (1 << bit)) for i in reached])
                value = jnp.where((me >> bit) & 1 == 1, got, value[:half])
                reached += [i | (1 << bit) for i in reached]
            parts.append(value)
        group = jnp.where(used, rows // 8, -1 - slot_index)
        same = group[:, None] == group[None, :]
        lead = used & ~jnp.any(same & (slot_index[None, :] < slot_index[:, None]), axis=1)
        lead_rank = jnp.sum(lead[None, :] & (slot_index[None, :] < slot_index[:, None]), axis=1)
        at = jnp.sum(jnp.where(same & lead[None, :], lead_rank[None, :], 0), axis=1)
        groups = jnp.sum(
            jnp.where(lead[None, :] & (lead_rank[None, :] == slot_index[:, None]), group[None, :], 0),
            axis=1)
        position = jnp.where(used, at * 8 + rows % 8, -1)
        spread = (jnp.arange(slots * 8)[:, None] == position[None, :]).astype(bf16)
        mask = jnp.max(spread, axis=1, keepdims=True)
        return parts, groups.astype(jnp.int32), jnp.sum(lead.astype(jnp.int32)), spread, mask

    pivot_rows, pivot_head = pivot_exchange(0)

    def more_pivots(state):
        turn, rows_, head_ = state
        extra_rows, extra_head = pivot_exchange(turn)
        return turn + 1, rows_ + extra_rows, head_ + extra_head

    _, pivot_rows, pivot_head = lax.while_loop(
        lambda s: s[0] < rounds, more_pivots, (jnp.int32(1), pivot_rows, pivot_head))

    upper = pivot_head[:panel, panel:]
    l_top = centred(dot(pivot_head[panel:, :panel], inverse_first)).astype(bf16)
    small = [inverse_first, inverse_second, upper, l_top]

    chunks = 5 if height % 5 == 0 else 1
    rows = height // chunks
    tile = 256 if rows % 256 == 0 else 128
    info = jnp.stack([first_row, row, jnp.int32(0)]).astype(jnp.int32)
    out = None
    pieces = []
    for k in range(chunks):
        pieces.append(along_row(matrix[k * rows : (k + 1) * rows, :pivots]))
    for k, piece in enumerate(pieces):
        out = update(info, k * rows, rows, tile, piece, matrix, pivot_rows, [pivot_head, *small], out)

    top_panel = jnp.concatenate(pieces[: -(-pivots // rows)], axis=0)[:pivots]

    def merged(turn, out):
        parts, groups, used, spread, mask = swapped_out(turn, top_panel)
        info = jnp.stack([first_row, row, used]).astype(jnp.int32)
        return merge(info, groups, spread, mask, pivot_rows, small, parts, wide_spans, out)

    out = merged(0, out)
    _, out = lax.while_loop(
        lambda s: s[0] < rounds, lambda s: (s[0] + 1, merged(s[0], s[1])), (jnp.int32(1), out))
    return out


def solution(mesh):
    return jax.shard_map(
        local,
        mesh=mesh,
        in_specs=(P(("col", "depth"), "row"), P(), P(), P()),
        out_specs=P(("col", "depth"), "row"),
        check_vma=False,
    )
```

time: 1570 us -> 295 us (0.19)
  waiting for transfers between devices: 1150 us -> 93.1 us
  local copies, waits for them, and re-layouts: 176 us -> 30 us
  matrix products: 131 us -> 12.8 us
  Pallas kernels: 0 us -> 76.7 us
  other arithmetic: 88.1 us -> 18.7 us
  starting transfers between devices: 9.25 us -> 55.3 us
    unnamed x6 -> x0, waiting for transfers between devices: 572 us -> none
    psum x3 -> x0, waiting for transfers between devices: 533 us -> none  [the longest x1 410 us: local(): lax.psum(picked, ('col', 'depth')).astype(jnp.float32).astype(jnp.bfloat16)]
    dot_general x7 -> x5, matrix products: 131 us -> 12.8 us  [dot(): return jnp.dot(a, b, preferred_element_type=f32)]
    ppermute x0 -> x45, waiting for transfers between devices: none -> 93.1 us  [the longest x12 45.3 us: along_row(): got = lax.ppermute(value, 'row', pairs)]
    scatter x2 -> x0, local copies, waits for them, and re-layouts: 89.4 us -> none  [local(): matrix.at[destinations]]
    pallas_call x0 -> x7, Pallas kernels: none -> 76.7 us  [the longest x5 54.3 us: update(): pl.pallas_call(functools.partial(update_kernel, base_row, tile, step, out...]
    ppermute x0 -> x45, starting transfers between devices: none -> 55.3 us  [the longest x24 26.1 us: hop(): lax.ppermute(value, blocks_axes, [(i, i ^ 1 << bit) for i in range(count)])]
    select_n x4 -> x22, other arithmetic: 52.1 us -> 11.8 us  [the longest x9 5.69 us: swapped_out(): value = jnp.where(me >> bit & 1 == 1, got, value[:half])]
  transfers between devices with their start and end apart: 7 -> 45, of which waited for: 6 -> 19; matrix products, arithmetic and copies ran while one was open for 3% -> 13% of each run, Pallas kernels for 0% -> 19%
where the time goes in v1:
time: 295 us; the launch traced here: 290 us
  waiting for transfers between devices  93.1 us (32%)
  Pallas kernels  76.7 us (26%)
  starting transfers between devices  55.3 us (19%)
  local copies, waits for them, and re-layouts  30 us (10%)
  other arithmetic  18.7 us (6%)
  matrix products  12.8 us (4%)
  between operations  3.23 us (1%)
    pallas_call x5, Pallas kernels, update(): pl.pallas_call(functools.partial(update_kernel, base_row, tile, step, out...  54.3 us
    ppermute x12, waiting for transfers between devices, along_row(): got = lax.ppermute(value, 'row', pairs)  45.3 us
    ppermute x24, waiting for transfers between devices, hop(): lax.ppermute(value, blocks_axes, [(i, i ^ 1 << bit) for i in range(count)])  29.1 us
    ppermute x24, starting transfers between devices, hop(): lax.ppermute(value, blocks_axes, [(i, i ^ 1 << bit) for i in range(count)])  26.1 us
    ppermute x9, waiting for transfers between devices, swapped_out(): lax.ppermute(value[half:], blocks_axes, [(i, i | 1 << bit) for i in reach...  18.6 us
    ppermute x12, starting transfers between devices, along_row(): got = lax.ppermute(value, 'row', pairs)  16.6 us
    pallas_call x1, Pallas kernels, merge(): pl.pallas_call(functools.partial(merge_kernel, spans), out_shape=jax.Shap...  14.1 us
    gather x1, local copies, waits for them, and re-layouts, pivot_exchange(): picked = jnp.take(matrix, rows, axis=0, mode='clip')  13.9 us
  transfers between devices with their start and end apart: 45, of which 19 were waited for; matrix products, arithmetic and copies ran while one was open for 13% of the time, Pallas kernels for 19%

profile of v1, /device:TPU:26, one launch (start us, length us, event | category | flops | bytes accessed | tf_op | source)
XLA Modules:
  0.0 290.1 jit_solution(1724737532847465810)
XLA Ops:
  1.2 13.9 %gather_fusion.1 = bf16[96,5120]{1,0:T(8,128)(2,1)S(1)} fusion(bf16[2560,5120]{1,0:T(8,128)(2,1)} %m_ref.9, s32[1024]{0:T(1024)S(1)} %pad_clamp_fusion.1), kind=kCustom, calls=%fused_computation.1 | custom fusion | bytes 1966464 | tf_op jit(solution)/shard_map/jit(_take)/gather | solution.py:282
  16.7 7.2 %collective-permute-done.56 = bf16[96,512]{1,0:T(8,128)(2,1)S(1)} collective-permute-done((bf16[96,512]{1,0:T(8,128)(2,1)S(1)}, bf16[96,512]{1,0:T(8,128)(2,1)S(1)}, u32[]{:S(2)}, u32[]{:S(2)}) %collective-permute-start.56) | collective-permute-done | bytes 98336 | tf_op jit(solution)/shard_map/ppermute | solution.py:255
  24.0 1.5 collective-permute-start.57
  26.6 1.5 collective-permute-start.43
  28.1 1.7 collective-permute-start.58
  29.8 1.5 collective-permute-start.45
  31.3 3.4 %collective-permute-done.58 = bf16[96,512]{1,0:T(8,128)(2,1)S(1)} collective-permute-done((bf16[96,512]{1,0:T(8,128)(2,1)S(1)}, bf16[96,512]{1,0:T(8,128)(2,1)S(1)}, u32[]{:S(2)}, u32[]{:S(2)}) %collective-permute-start.58) | collective-permute-done | bytes 98336 | tf_op jit(solution)/shard_map/ppermute | solution.py:249
  34.7 1.5 collective-permute-start.38
  40.7 5.7 %collective-permute-done.38.refs_4_ = bf16[96,1664]{1,0:T(8,128)(2,1)S(1)} collective-permute-done((bf16[96,1664]{1,0:T(8,128)(2,1)S(1)}, bf16[96,1664]{1,0:T(8,128)(2,1)S(1)}, u32[]{:S(2)}, u32[]{:S(2)}) %collective-permute-start.38) | collective-permute-done | bytes 319520 | tf_op jit(solution)/shard_map/ppermute | solution.py:249
  48.4 1.5 collective-permute-start.37
  51.0 1.5 collective-permute-start.47
  53.0 1.6 collective-permute-start.60
  56.4 2.2 collective-permute-done.37.refs_3_
  60.0 1.6 collective-permute-done.47.refs_14_
  61.5 1.5 collective-permute-start.40
  63.1 5.2 %collective-permute-done.39.refs_5_ = bf16[96,1664]{1,0:T(8,128)(2,1)S(1)} collective-permute-done((bf16[96,1664]{1,0:T(8,128)(2,1)S(1)}, bf16[96,1664]{1,0:T(8,128)(2,1)S(1)}, u32[]{:S(2)}, u32[]{:S(2)}) %collective-permute-start.39) | collective-permute-done | bytes 319520 | tf_op jit(solution)/shard_map/ppermute | solution.py:249
  72.8 7.1 %collective-permute-done.40.refs_6_ = bf16[96,1664]{1,0:T(8,128)(2,1)S(1)} collective-permute-done((bf16[96,1664]{1,0:T(8,128)(2,1)S(1)}, bf16[96,1664]{1,0:T(8,128)(2,1)S(1)}, u32[]{:S(2)}, u32[]{:S(2)}) %collective-permute-start.40) | collective-permute-done | bytes 319520 | tf_op jit(solution)/shard_map/ppermute | solution.py:249
  81.9 1.5 collective-permute-start.41
  84.5 1.5 collective-permute-start.55
  86.3 1.9 slice.266
  90.1 2.7 fusion.42
  92.9 1.7 collective-permute-done.55.refs_23_
  94.7 8.3 %place.6 = bf16[512,5120]{1,0:T(8,128)(2,1)} custom-call(bf16[512,768]{1,0:T(8,128)(2,1)S(1)} %fusion.41.onehot_ref, bf16[96,1664]{1,0:T(8,128)(2,1)S(1)} %get-tuple-element.740.refs_0_, bf16[96,1664]{1,0:T(8,128)(2,1)S(1)} %copy-done.21, bf16[96,1664]{1,0:T(8,128)(2,1)S(1)} %copy-done.23, bf16[96,1664]{1,0:T(8,128)(2,1)} %collective-permute-done.37.refs_3_, ...), custom_call_target="tpu_custom_call" | custom-call | tf_op jit(solution)/shard_map/place/pallas_call | solution.py:71
  104.7 3.1 %convolution_convert_fusion.5 = bf16[768,1792]{1,0:T(8,128)(2,1)S(1)} fusion(bf16[2560,5120]{1,0:T(8,128)(2,1)} %get-tuple-element.1136, s32[512]{0:T(512)S(1)} %get-tuple-element.743), kind=kOutput, calls=%fused_computation.97 | convolution fusion | flops 1411055616 | bytes 4589568 | tf_op jit(solution)/shard_map/dot_general | solution.py:18
  107.8 1.6 copy-done.51
  110.6 1.8 collective-permute-start.61
  114.1 4.9 %convolution_convert_fusion.4 = bf16[768,1920]{1,0:T(8,128)(2,1)} fusion(bf16[2560,5120]{1,0:T(8,128)(2,1)} %get-tuple-element.1136, s32[512]{0:T(512)S(1)} %get-tuple-element.742), kind=kOutput, calls=%fused_computation.96 | convolution fusion | flops 1511817216 | bytes 4917248 | tf_op jit(solution)/shard_map/dot_general | solution.py:18
  119.0 2.1 collective-permute-done.78
  121.2 2.9 %broadcast_select_fusion.2 = (bf16[512,512]{1,0:T(8,128)(2,1)S(1)}, bf16[512,512]{1,0:T(8,128)(2,1)}, bf16[512,512]{1,0:T(8,128)(2,1)}, bf16[512,512]{1,0:T(8,128)(2,1)}, bf16[512,512]{1,0:T(8,128)(2,1)S(1)}) fusion(bf16[512,512]{1,0:T(8,128)(2,1)S(1)} %collective-permute-done.78, pred[]{:T(512)} %eq.452, bf16[2560,5120]{1,0:T(8,128)(2,1)} %get-tuple-element.1136), kind=kLoop, calls=%fused_computation.128 | loop fusion | flops 262144 | bytes 5767169 | tf_op jit(solution)/shard_map/jit(_where)/select_n | solution.py:256
  126.9 1.5 slice.347
  134.1 22.7 %collective-permute-done.67 = bf16[512,512]{1,0:T(8,128)(2,1)S(1)} collective-permute-done((bf16[512,512]{1,0:T(8,128)(2,1)S(1)}, bf16[512,512]{1,0:T(8,128)(2,1)S(1)}, u32[]{:S(2)}, u32[]{:S(2)}) %collective-permute-start.67) | collective-permute-done | bytes 524320 | tf_op jit(solution)/shard_map/ppermute | solution.py:255
  158.9 3.5 %collective-permute-done.72 = bf16[512,512]{1,0:T(8,128)(2,1)S(1)} collective-permute-done((bf16[512,512]{1,0:T(8,128)(2,1)}, bf16[512,512]{1,0:T(8,128)(2,1)S(1)}, u32[]{:S(2)}, u32[]{:S(2)}) %collective-permute-start.72) | collective-permute-done | bytes 524320 | tf_op jit(solution)/shard_map/ppermute | solution.py:255
  164.0 4.1 %collective-permute-done.74 = bf16[512,512]{1,0:T(8,128)(2,1)S(1)} collective-permute-done((bf16[512,512]{1,0:T(8,128)(2,1)}, bf16[512,512]{1,0:T(8,128)(2,1)S(1)}, u32[]{:S(2)}, u32[]{:S(2)}) %collective-permute-start.74) | collective-permute-done | bytes 524320 | tf_op jit(solution)/shard_map/ppermute | solution.py:255
  168.1 5.6 %collective-permute-done.76 = bf16[512,512]{1,0:T(8,128)(2,1)S(1)} collective-permute-done((bf16[512,512]{1,0:T(8,128)(2,1)}, bf16[512,512]{1,0:T(8,128)(2,1)S(1)}, u32[]{:S(2)}, u32[]{:S(2)}) %collective-permute-start.76) | collective-permute-done | bytes 524320 | tf_op jit(solution)/shard_map/ppermute | solution.py:255
  173.7 1.9 broadcast_select_fusion.3
  178.4 2.1 collective-permute-start.75
  180.5 1.7 slice_select_fusion.11
  186.2 1.8 convolution_convert_fusion.3
  188.0 11.0 %update.5.rest_0_ = bf16[2560,5120]{1,0:T(8,128)(2,1)} custom-call(s32[3]{0:T(128)S(1)} %pad_add_fusion.3.info, bf16[512,512]{1,0:T(8,128)(2,1)S(1)} %broadcast_select_fusion.11.a_ref, bf16[2560,5120]{1,0:T(8,128)(2,1)} %get-tuple-element.1136, bf16[512,5120]{1,0:T(8,128)(2,1)} %get-tuple-element.1018.p_ref, bf16[512,512]{1,0:T(8,128)(2,1)S(1)} %copy-done.46, ...), custom_call_target="tpu_custom_call" | custom-call | flops 2684354560 | bytes 10485760 | tf_op jit(solution)/shard_map/update/pallas_call | solution.py:129
  199.1 10.8 %update.6.rest_0_ = bf16[2560,5120]{1,0:T(8,128)(2,1)} custom-call(s32[3]{0:T(128)S(1)} %pad_add_fusion.3.info, bf16[512,512]{1,0:T(8,128)(2,1)S(1)} %broadcast_select_fusion.7.a_ref, bf16[2560,5120]{1,0:T(8,128)(2,1)} %get-tuple-element.1136, bf16[512,5120]{1,0:T(8,128)(2,1)} %get-tuple-element.1018.p_ref, ...), custom_call_target="tpu_custom_call", output_to_operand_aliasing={{}: (9, {})} | custom-call | flops 2684354560 | bytes 10485760 | tf_op jit(solution)/shard_map/update/pallas_call | solution.py:129
  211.8 10.8 %update.7.rest_0_ = bf16[2560,5120]{1,0:T(8,128)(2,1)} custom-call(s32[3]{0:T(128)S(1)} %pad_add_fusion.3.info, bf16[512,512]{1,0:T(8,128)(2,1)S(1)} %broadcast_select_fusion.8.a_ref, bf16[2560,5120]{1,0:T(8,128)(2,1)} %get-tuple-element.1136, bf16[512,5120]{1,0:T(8,128)(2,1)} %get-tuple-element.1018.p_ref, ...), custom_call_target="tpu_custom_call", output_to_operand_aliasing={{}: (9, {})} | custom-call | flops 2684354560 | bytes 10485760 | tf_op jit(solution)/shard_map/update/pallas_call | solution.py:129
  222.7 10.8 %update.8.rest_0_ = bf16[2560,5120]{1,0:T(8,128)(2,1)} custom-call(s32[3]{0:T(128)S(1)} %pad_add_fusion.3.info, bf16[512,512]{1,0:T(8,128)(2,1)S(1)} %broadcast_select_fusion.9.a_ref, bf16[2560,5120]{1,0:T(8,128)(2,1)} %get-tuple-element.1136, bf16[512,5120]{1,0:T(8,128)(2,1)} %get-tuple-element.1018.p_ref, ...), custom_call_target="tpu_custom_call", output_to_operand_aliasing={{}: (9, {})} | custom-call | flops 2684354560 | bytes 10485760 | tf_op jit(solution)/shard_map/update/pallas_call | solution.py:129
  233.5 10.8 %update.9.rest_3_ = bf16[2560,5120]{1,0:T(8,128)(2,1)} custom-call(s32[3]{0:T(128)S(1)} %pad_add_fusion.3.info, bf16[512,512]{1,0:T(8,128)(2,1)S(1)} %broadcast_select_fusion.10.a_ref, bf16[2560,5120]{1,0:T(8,128)(2,1)} %get-tuple-element.1136, bf16[512,5120]{1,0:T(8,128)(2,1)} %get-tuple-element.1018.p_ref, ...), custom_call_target="tpu_custom_call", output_to_operand_aliasing={{}: (9, {})} | custom-call | flops 2684354560 | bytes 10485760 | tf_op jit(solution)/shard_map/update/pallas_call | solution.py:129
  247.0 3.7 %collective-permute-start.63 = (bf16[96,1792]{1,0:T(8,128)(2,1)S(1)}, bf16[96,1792]{1,0:T(8,128)(2,1)S(1)}, u32[]{:S(2)}, u32[]{:S(2)}) collective-permute-start(bf16[96,1792]{1,0:T(8,128)(2,1)S(1)} %slice.345), channel_id=1, source_target_pairs={{0,4},{1,5},{2,6},{3,7},{8,12},{9,13},{10,14},{11,15},{16,20},{17,... | collective-permute-start | bytes 1032200 | tf_op jit(solution)/shard_map/ppermute | solution.py:311
  253.1 2.3 collective-permute-done.63
  257.6 3.6 %collective-permute-done.66 = bf16[96,1920]{1,0:T(8,128)(2,1)S(1)} collective-permute-done((bf16[96,1920]{1,0:T(8,128)(2,1)S(1)}, bf16[96,1920]{1,0:T(8,128)(2,1)S(1)}, u32[]{:S(2)}, u32[]{:S(2)}) %collective-permute-start.66) | collective-permute-done | bytes 368672 | tf_op jit(solution)/shard_map/ppermute | solution.py:311
  262.0 12.7 %collective-permute-done.71 = bf16[96,1920]{1,0:T(8,128)(2,1)S(1)} collective-permute-done((bf16[96,1920]{1,0:T(8,128)(2,1)S(1)}, bf16[96,1920]{1,0:T(8,128)(2,1)S(1)}, u32[]{:S(2)}, u32[]{:S(2)}) %collective-permute-start.71) | collective-permute-done | bytes 368672 | tf_op jit(solution)/shard_map/ppermute | solution.py:311
  275.5 14.1 %merge.5 = bf16[2560,5120]{1,0:T(8,128)(2,1)} custom-call(s32[3]{0:T(128)} %pad_add_fusion.1.info, s32[96]{0:T(128)} %get-tuple-element.655.groups, bf16[768,96]{1,0:T(8,128)(2,1)} %fusion.55.spread_ref, bf16[768,1]{1,0:T(8,128)(2,1)} %broadcast_in_dim.238.mask_ref, bf16[512,5120]{1,0:T(8,128)(2,1)} %get-tuple-element.1018.p_ref, ...), custom_call_target="tpu_custom_call", output_to_operand_aliasing={{}: (12, {})} | custom-call | flops 1006632960 | bytes 15728640 | tf_op jit(solution)/shard_map/merge/pallas_call | solution.py:210
  (187 shorter events, 56.9 us)
Async XLA Ops:
  15.4 8.5 %collective-permute-start.56 = (bf16[96,512]{1,0:T(8,128)(2,1)S(1)}, bf16[96,512]{1,0:T(8,128)(2,1)S(1)}, u32[]{:S(2)}, u32[]{:S(2)}) collective-permute-start(bf16[96,512]{1,0:T(8,128)(2,1)S(1)} %slice.340), channel_id=1, source_target_pairs={{0,16},{1,17},{2,18},{3,19},{4,20},{5,21},{6,22},{7,23}} | collective-permute-start | bytes 294920 | tf_op jit(solution)/shard_map/ppermute | solution.py:255
  24.0 4.1 %collective-permute-start.57 = (bf16[96,512]{1,0:T(8,128)(2,1)S(1)}, bf16[96,512]{1,0:T(8,128)(2,1)S(1)}, u32[]{:S(2)}, u32[]{:S(2)}) collective-permute-start(bf16[96,512]{1,0:T(8,128)(2,1)S(1)} %broadcast_select_fusion.12), channel_id=1, source_target_pairs={{0,8},{16,24},{1,9},{17,25},{2,10},{18,26},{3,11},{19,27},{4,12},{... | collective-permute-start | bytes 294920 | tf_op jit(solution)/shard_map/ppermute | solution.py:255
  25.5 11.7 %collective-permute-start.35 = (bf16[96,1664]{1,0:T(8,128)(2,1)S(1)}, bf16[96,1664]{1,0:T(8,128)(2,1)S(1)}, u32[]{:S(2)}, u32[]{:S(2)}) collective-permute-start(bf16[96,1664]{1,0:T(8,128)(2,1)S(1)} %get-tuple-element.740.refs_0_), channel_id=1, source_target_pairs={{0,1},{1,0},{2,3},{3,2},{4,5},{5,4},{6,7},{7,6},{8,9},{9,8},{10,11... | collective-permute-start | bytes 958472 | tf_op jit(solution)/shard_map/ppermute | solution.py:249
  26.0 12.2 %collective-permute-start.36 = (bf16[96,1664]{1,0:T(8,128)(2,1)S(1)}, bf16[96,1664]{1,0:T(8,128)(2,1)S(1)}, u32[]{:S(2)}, u32[]{:S(2)}) collective-permute-start(bf16[96,1664]{1,0:T(8,128)(2,1)S(1)} %get-tuple-element.740.refs_0_), channel_id=1, source_target_pairs={{0,2},{1,3},{2,0},{3,1},{4,6},{5,7},{6,4},{7,5},{8,10},{9,11},{10,... | collective-permute-start | bytes 958472 | tf_op jit(solution)/shard_map/ppermute | solution.py:249
  26.6 11.2 %collective-permute-start.43 = (bf16[96,1664]{1,0:T(8,128)(2,1)S(1)}, bf16[96,1664]{1,0:T(8,128)(2,1)S(1)}, u32[]{:S(2)}, u32[]{:S(2)}) collective-permute-start(bf16[96,1664]{1,0:T(8,128)(2,1)S(1)} %get-tuple-element.739.refs_8_), channel_id=1, source_target_pairs={{0,2},{1,3},{2,0},{3,1},{4,6},{5,7},{6,4},{7,5},{8,10},{9,11},{10,... | collective-permute-start | bytes 958472 | tf_op jit(solution)/shard_map/ppermute | solution.py:249
  28.1 57.9 %copy-start.56 = (bf16[96,512]{1,0:T(8,128)(2,1)}, bf16[96,512]{1,0:T(8,128)(2,1)S(1)}, u32[]{:S(2)}) copy-start(bf16[96,512]{1,0:T(8,128)(2,1)S(1)} %broadcast_select_fusion.13) | copy-start | bytes 294916
  28.1 6.6 %collective-permute-start.58 = (bf16[96,512]{1,0:T(8,128)(2,1)S(1)}, bf16[96,512]{1,0:T(8,128)(2,1)S(1)}, u32[]{:S(2)}, u32[]{:S(2)}) collective-permute-start(bf16[96,512]{1,0:T(8,128)(2,1)S(1)} %broadcast_select_fusion.13), channel_id=1, source_target_pairs={{0,1},{1,0},{2,3},{3,2},{4,5},{5,4},{6,7},{7,6},{8,9},{9,8},{10,11... | collective-permute-start | bytes 294920 | tf_op jit(solution)/shard_map/ppermute | solution.py:249
  29.8 9.7 %collective-permute-start.45 = (bf16[96,1664]{1,0:T(8,128)(2,1)S(1)}, bf16[96,1664]{1,0:T(8,128)(2,1)S(1)}, u32[]{:S(2)}, u32[]{:S(2)}) collective-permute-start(bf16[96,1664]{1,0:T(8,128)(2,1)S(1)} %get-tuple-element.739.refs_8_), channel_id=1, source_target_pairs={{0,4},{1,5},{2,6},{3,7},{4,0},{5,1},{6,2},{7,3},{8,12},{9,13},{10,... | collective-permute-start | bytes 958472 | tf_op jit(solution)/shard_map/ppermute | solution.py:249
  34.7 51.3 %copy-start.59 = (bf16[96,512]{1,0:T(8,128)(2,1)}, bf16[96,512]{1,0:T(8,128)(2,1)S(1)}, u32[]{:S(2)}) copy-start(bf16[96,512]{1,0:T(8,128)(2,1)S(1)} %collective-permute-done.58) | copy-start | bytes 294916
  34.7 11.6 %collective-permute-start.38 = (bf16[96,1664]{1,0:T(8,128)(2,1)S(1)}, bf16[96,1664]{1,0:T(8,128)(2,1)S(1)}, u32[]{:S(2)}, u32[]{:S(2)}) collective-permute-start(bf16[96,1664]{1,0:T(8,128)(2,1)S(1)} %get-tuple-element.740.refs_0_), channel_id=1, source_target_pairs={{0,4},{1,5},{2,6},{3,7},{4,0},{5,1},{6,2},{7,3},{8,12},{9,13},{10,... | collective-permute-start | bytes 958472 | tf_op jit(solution)/shard_map/ppermute | solution.py:249
  37.2 48.8 %copy-start.20 = (bf16[96,1664]{1,0:T(8,128)(2,1)}, bf16[96,1664]{1,0:T(8,128)(2,1)S(1)}, u32[]{:S(2)}) copy-start(bf16[96,1664]{1,0:T(8,128)(2,1)S(1)} %collective-permute-done.35.refs_1_) | copy-start | bytes 958468
  37.3 13.7 %collective-permute-start.52 = (bf16[96,1792]{1,0:T(8,128)(2,1)S(1)}, bf16[96,1792]{1,0:T(8,128)(2,1)S(1)}, u32[]{:S(2)}, u32[]{:S(2)}) collective-permute-start(bf16[96,1792]{1,0:T(8,128)(2,1)S(1)} %slice.339.refs_16_), channel_id=1, source_target_pairs={{0,4},{1,5},{2,6},{3,7},{4,0},{5,1},{6,2},{7,3},{8,12},{9,13},{10,... | collective-permute-start | bytes 1032200 | tf_op jit(solution)/shard_map/ppermute | solution.py:249
  37.8 9.8 %collective-permute-start.42 = (bf16[96,1664]{1,0:T(8,128)(2,1)S(1)}, bf16[96,1664]{1,0:T(8,128)(2,1)S(1)}, u32[]{:S(2)}, u32[]{:S(2)}) collective-permute-start(bf16[96,1664]{1,0:T(8,128)(2,1)S(1)} %get-tuple-element.739.refs_8_), channel_id=1, source_target_pairs={{0,1},{1,0},{2,3},{3,2},{4,5},{5,4},{6,7},{7,6},{8,9},{9,8},{10,11... | collective-permute-start | bytes 958472 | tf_op jit(solution)/shard_map/ppermute | solution.py:249
  38.3 14.2 %collective-permute-start.59 = (bf16[192,512]{1,0:T(8,128)(2,1)S(1)}, bf16[192,512]{1,0:T(8,128)(2,1)S(1)}, u32[]{:S(2)}, u32[]{:S(2)}) collective-permute-start(bf16[192,512]{1,0:T(8,128)(2,1)S(1)} %pad_maximum_fusion.4), channel_id=1, source_target_pairs={{0,2},{1,3},{2,0},{3,1},{4,6},{5,7},{6,4},{7,5},{8,10},{9,11},{10,... | collective-permute-start | bytes 589832 | tf_op jit(solution)/shard_map/ppermute | solution.py:249
  39.5 13.6 %collective-permute-start.49 = (bf16[96,1792]{1,0:T(8,128)(2,1)S(1)}, bf16[96,1792]{1,0:T(8,128)(2,1)S(1)}, u32[]{:S(2)}, u32[]{:S(2)}) collective-permute-start(bf16[96,1792]{1,0:T(8,128)(2,1)S(1)} %slice.339.refs_16_), channel_id=1, source_target_pairs={{0,1},{1,0},{2,3},{3,2},{4,5},{5,4},{6,7},{7,6},{8,9},{9,8},{10,11... | collective-permute-start | bytes 1032200 | tf_op jit(solution)/shard_map/ppermute | solution.py:249
  47.1 8.0 %collective-permute-start.50 = (bf16[96,1792]{1,0:T(8,128)(2,1)S(1)}, bf16[96,1792]{1,0:T(8,128)(2,1)S(1)}, u32[]{:S(2)}, u32[]{:S(2)}) collective-permute-start(bf16[96,1792]{1,0:T(8,128)(2,1)S(1)} %slice.339.refs_16_), channel_id=1, source_target_pairs={{0,2},{1,3},{2,0},{3,1},{4,6},{5,7},{6,4},{7,5},{8,10},{9,11},{10,... | collective-permute-start | bytes 1032200 | tf_op jit(solution)/shard_map/ppermute | solution.py:249
  48.4 10.3 %collective-permute-start.37 = (bf16[96,1664]{1,0:T(8,128)(2,1)S(1)}, bf16[96,1664]{1,0:T(8,128)(2,1)}, u32[]{:S(2)}, u32[]{:S(2)}) collective-permute-start(bf16[96,1664]{1,0:T(8,128)(2,1)S(1)} %collective-permute-done.35.refs_1_), channel_id=1, source_target_pairs={{0,2},{1,3},{2,0},{3,1},{4,6},{5,7},{6,4},{7,5},{8,10},{9,11},{10,... | collective-permute-start | bytes 958472 | tf_op jit(solution)/shard_map/ppermute | solution.py:249
  51.0 10.6 %collective-permute-start.47 = (bf16[96,1664]{1,0:T(8,128)(2,1)S(1)}, bf16[96,1664]{1,0:T(8,128)(2,1)}, u32[]{:S(2)}, u32[]{:S(2)}) collective-permute-start(bf16[96,1664]{1,0:T(8,128)(2,1)S(1)} %collective-permute-done.43.refs_10_), channel_id=1, source_target_pairs={{0,4},{1,5},{2,6},{3,7},{4,0},{5,1},{6,2},{7,3},{8,12},{9,13},{10,... | collective-permute-start | bytes 958472 | tf_op jit(solution)/shard_map/ppermute | solution.py:249
  52.5 15.8 %collective-permute-start.39 = (bf16[96,1664]{1,0:T(8,128)(2,1)S(1)}, bf16[96,1664]{1,0:T(8,128)(2,1)S(1)}, u32[]{:S(2)}, u32[]{:S(2)}) collective-permute-start(bf16[96,1664]{1,0:T(8,128)(2,1)S(1)} %collective-permute-done.35.refs_1_), channel_id=1, source_target_pairs={{0,4},{1,5},{2,6},{3,7},{4,0},{5,1},{6,2},{7,3},{8,12},{9,13},{10,... | collective-permute-start | bytes 958472 | tf_op jit(solution)/shard_map/ppermute | solution.py:249
  53.0 31.5 %collective-permute-start.60 = (bf16[384,512]{1,0:T(8,128)(2,1)S(1)}, bf16[384,512]{1,0:T(8,128)(2,1)S(1)}, u32[]{:S(2)}, u32[]{:S(2)}) collective-permute-start(bf16[384,512]{1,0:T(8,128)(2,1)S(1)} %pad_maximum_fusion.3), channel_id=1, source_target_pairs={{0,4},{1,5},{2,6},{3,7},{4,0},{5,1},{6,2},{7,3},{8,12},{9,13},{10,... | collective-permute-start | bytes 1179656 | tf_op jit(solution)/shard_map/ppermute | solution.py:249
  55.1 28.3 %collective-permute-start.53 = (bf16[96,1792]{1,0:T(8,128)(2,1)S(1)}, bf16[96,1792]{1,0:T(8,128)(2,1)S(1)}, u32[]{:S(2)}, u32[]{:S(2)}) collective-permute-start(bf16[96,1792]{1,0:T(8,128)(2,1)S(1)} %collective-permute-done.52.refs_20_), channel_id=1, source_target_pairs={{0,1},{1,0},{2,3},{3,2},{4,5},{5,4},{6,7},{7,6},{8,9},{9,8},{10,11... | collective-permute-start | bytes 1032200 | tf_op jit(solution)/shard_map/ppermute | solution.py:249
  58.7 12.9 %collective-permute-start.44 = (bf16[96,1664]{1,0:T(8,128)(2,1)S(1)}, bf16[96,1664]{1,0:T(8,128)(2,1)S(1)}, u32[]{:S(2)}, u32[]{:S(2)}) collective-permute-start(bf16[96,1664]{1,0:T(8,128)(2,1)S(1)} %collective-permute-done.43.refs_10_), channel_id=1, source_target_pairs={{0,1},{1,0},{2,3},{3,2},{4,5},{5,4},{6,7},{7,6},{8,9},{9,8},{10,11... | collective-permute-start | bytes 958472 | tf_op jit(solution)/shard_map/ppermute | solution.py:249
  61.5 18.4 %collective-permute-start.40 = (bf16[96,1664]{1,0:T(8,128)(2,1)S(1)}, bf16[96,1664]{1,0:T(8,128)(2,1)S(1)}, u32[]{:S(2)}, u32[]{:S(2)}) collective-permute-start(bf16[96,1664]{1,0:T(8,128)(2,1)S(1)} %collective-permute-done.36.refs_2_), channel_id=1, source_target_pairs={{0,4},{1,5},{2,6},{3,7},{4,0},{5,1},{6,2},{7,3},{8,12},{9,13},{10,... | collective-permute-start | bytes 958472 | tf_op jit(solution)/shard_map/ppermute | solution.py:249
  69.0 12.2 %collective-permute-start.46 = (bf16[96,1664]{1,0:T(8,128)(2,1)S(1)}, bf16[96,1664]{1,0:T(8,128)(2,1)S(1)}, u32[]{:S(2)}, u32[]{:S(2)}) collective-permute-start(bf16[96,1664]{1,0:T(8,128)(2,1)S(1)} %collective-permute-done.45.refs_12_), channel_id=1, source_target_pairs={{0,1},{1,0},{2,3},{3,2},{4,5},{5,4},{6,7},{7,6},{8,9},{9,8},{10,11... | collective-permute-start | bytes 958472 | tf_op jit(solution)/shard_map/ppermute | solution.py:249
  72.3 20.6 %collective-permute-start.54 = (bf16[96,1792]{1,0:T(8,128)(2,1)S(1)}, bf16[96,1792]{1,0:T(8,128)(2,1)S(1)}, u32[]{:S(2)}, u32[]{:S(2)}) collective-permute-start(bf16[96,1792]{1,0:T(8,128)(2,1)S(1)} %collective-permute-done.52.refs_20_), channel_id=1, source_target_pairs={{0,2},{1,3},{2,0},{3,1},{4,6},{5,7},{6,4},{7,5},{8,10},{9,11},{10,... | collective-permute-start | bytes 1032200 | tf_op jit(solution)/shard_map/ppermute | solution.py:249
  80.7 12.2 %collective-permute-start.51 = (bf16[96,1792]{1,0:T(8,128)(2,1)S(1)}, bf16[96,1792]{1,0:T(8,128)(2,1)}, u32[]{:S(2)}, u32[]{:S(2)}) collective-permute-start(bf16[96,1792]{1,0:T(8,128)(2,1)S(1)} %collective-permute-done.49.refs_17_), channel_id=1, source_target_pairs={{0,2},{1,3},{2,0},{3,1},{4,6},{5,7},{6,4},{7,5},{8,10},{9,11},{10,... | collective-permute-start | bytes 1032200 | tf_op jit(solution)/shard_map/ppermute | solution.py:249
  81.9 11.0 %collective-permute-start.41 = (bf16[96,1664]{1,0:T(8,128)(2,1)}, bf16[96,1664]{1,0:T(8,128)(2,1)}, u32[]{:S(2)}, u32[]{:S(2)}) collective-permute-start(bf16[96,1664]{1,0:T(8,128)(2,1)} %collective-permute-done.37.refs_3_), channel_id=1, source_target_pairs={{0,4},{1,5},{2,6},{3,7},{4,0},{5,1},{6,2},{7,3},{8,12},{9,13},{10,... | collective-permute-start | bytes 958472 | tf_op jit(solution)/shard_map/ppermute | solution.py:249
  83.4 9.5 %collective-permute-start.48 = (bf16[96,1664]{1,0:T(8,128)(2,1)}, bf16[96,1664]{1,0:T(8,128)(2,1)}, u32[]{:S(2)}, u32[]{:S(2)}) collective-permute-start(bf16[96,1664]{1,0:T(8,128)(2,1)} %collective-permute-done.47.refs_14_), channel_id=1, source_target_pairs={{0,1},{1,0},{2,3},{3,2},{4,5},{5,4},{6,7},{7,6},{8,9},{9,8},{10,11... | collective-permute-start | bytes 958472 | tf_op jit(solution)/shard_map/ppermute | solution.py:249
  84.5 10.1 %collective-permute-start.55 = (bf16[96,1792]{1,0:T(8,128)(2,1)S(1)}, bf16[96,1792]{1,0:T(8,128)(2,1)}, u32[]{:S(2)}, u32[]{:S(2)}) collective-permute-start(bf16[96,1792]{1,0:T(8,128)(2,1)S(1)} %collective-permute-done.53.refs_21_), channel_id=1, source_target_pairs={{0,2},{1,3},{2,0},{3,1},{4,6},{5,7},{6,4},{7,5},{8,10},{9,11},{10,... | collective-permute-start | bytes 1032200 | tf_op jit(solution)/shard_map/ppermute | solution.py:249
  103.4 17.8 %collective-permute-start.78 = (bf16[512,512]{1,0:T(8,128)(2,1)}, bf16[512,512]{1,0:T(8,128)(2,1)S(1)}, u32[]{:S(2)}, u32[]{:S(2)}) collective-permute-start(bf16[512,512]{1,0:T(8,128)(2,1)} %slice.266), channel_id=1, source_target_pairs={{0,16},{1,17},{2,18},{3,19},{4,20},{5,21},{6,22},{7,23}} | collective-permute-start | bytes 1572872 | tf_op jit(solution)/shard_map/ppermute | solution.py:255
  110.6 69.9 %collective-permute-start.61 = (bf16[384,1792]{1,0:T(8,128)(2,1)}, bf16[384,1792]{1,0:T(8,128)(2,1)}, u32[]{:S(2)}, u32[]{:S(2)}) collective-permute-start(bf16[384,1792]{1,0:T(8,128)(2,1)} %slice.341), channel_id=1, source_target_pairs={{0,1},{8,9},{16,17},{24,25}} | collective-permute-start | bytes 4128776 | tf_op jit(solution)/shard_map/ppermute | solution.py:311
  124.1 32.8 %collective-permute-start.67 = (bf16[512,512]{1,0:T(8,128)(2,1)S(1)}, bf16[512,512]{1,0:T(8,128)(2,1)S(1)}, u32[]{:S(2)}, u32[]{:S(2)}) collective-permute-start(bf16[512,512]{1,0:T(8,128)(2,1)S(1)} %get-tuple-element.734), channel_id=1, source_target_pairs={{0,16},{1,17},{2,18},{3,19},{4,20},{5,21},{6,22},{7,23}} | collective-permute-start | bytes 1572872 | tf_op jit(solution)/shard_map/ppermute | solution.py:255
  128.4 34.0 %collective-permute-start.72 = (bf16[512,512]{1,0:T(8,128)(2,1)}, bf16[512,512]{1,0:T(8,128)(2,1)S(1)}, u32[]{:S(2)}, u32[]{:S(2)}) collective-permute-start(bf16[512,512]{1,0:T(8,128)(2,1)} %get-tuple-element.733), channel_id=1, source_target_pairs={{0,16},{1,17},{2,18},{3,19},{4,20},{5,21},{6,22},{7,23}} | collective-permute-start | bytes 1572872 | tf_op jit(solution)/shard_map/ppermute | solution.py:255
  130.8 37.3 %collective-permute-start.74 = (bf16[512,512]{1,0:T(8,128)(2,1)}, bf16[512,512]{1,0:T(8,128)(2,1)S(1)}, u32[]{:S(2)}, u32[]{:S(2)}) collective-permute-start(bf16[512,512]{1,0:T(8,128)(2,1)} %get-tuple-element.732), channel_id=1, source_target_pairs={{0,16},{1,17},{2,18},{3,19},{4,20},{5,21},{6,22},{7,23}} | collective-permute-start | bytes 1572872 | tf_op jit(solution)/shard_map/ppermute | solution.py:255
  132.1 41.6 %collective-permute-start.76 = (bf16[512,512]{1,0:T(8,128)(2,1)}, bf16[512,512]{1,0:T(8,128)(2,1)S(1)}, u32[]{:S(2)}, u32[]{:S(2)}) collective-permute-start(bf16[512,512]{1,0:T(8,128)(2,1)} %get-tuple-element.731), channel_id=1, source_target_pairs={{0,16},{1,17},{2,18},{3,19},{4,20},{5,21},{6,22},{7,23}} | collective-permute-start | bytes 1572872 | tf_op jit(solution)/shard_map/ppermute | solution.py:255
  156.8 26.7 %collective-permute-start.64 = (bf16[384,1920]{1,0:T(8,128)(2,1)S(1)}, bf16[384,1920]{1,0:T(8,128)(2,1)S(1)}, u32[]{:S(2)}, u32[]{:S(2)}) collective-permute-start(bf16[384,1920]{1,0:T(8,128)(2,1)S(1)} %slice.347), channel_id=1, source_target_pairs={{0,2},{8,10},{16,18},{24,26}} | collective-permute-start | bytes 4423688 | tf_op jit(solution)/shard_map/ppermute | solution.py:311
  162.4 15.8 %collective-permute-start.79 = (bf16[512,512]{1,0:T(8,128)(2,1)S(1)}, bf16[512,512]{1,0:T(8,128)(2,1)S(1)}, u32[]{:S(2)}, u32[]{:S(2)}) collective-permute-start(bf16[512,512]{1,0:T(8,128)(2,1)S(1)} %get-tuple-element.730), channel_id=1, source_target_pairs={{0,8},{16,24},{1,9},{17,25},{2,10},{18,26},{3,11},{19,27},{4,12},{... | collective-permute-start | bytes 1572872 | tf_op jit(solution)/shard_map/ppermute | solution.py:255
  175.6 10.5 %collective-permute-start.68 = (bf16[512,512]{1,0:T(8,128)(2,1)S(1)}, bf16[512,512]{1,0:T(8,128)(2,1)S(1)}, u32[]{:S(2)}, u32[]{:S(2)}) collective-permute-start(bf16[512,512]{1,0:T(8,128)(2,1)S(1)} %get-tuple-element.738), channel_id=1, source_target_pairs={{0,8},{16,24},{1,9},{17,25},{2,10},{18,26},{3,11},{19,27},{4,12},{... | collective-permute-start | bytes 1572872 | tf_op jit(solution)/shard_map/ppermute | solution.py:255
  177.0 33.7 %collective-permute-start.77 = (bf16[512,512]{1,0:T(8,128)(2,1)S(1)}, bf16[512,512]{1,0:T(8,128)(2,1)S(1)}, u32[]{:S(2)}, u32[]{:S(2)}) collective-permute-start(bf16[512,512]{1,0:T(8,128)(2,1)S(1)} %get-tuple-element.735), channel_id=1, source_target_pairs={{0,8},{16,24},{1,9},{17,25},{2,10},{18,26},{3,11},{19,27},{4,12},{... | collective-permute-start | bytes 1572872 | tf_op jit(solution)/shard_map/ppermute | solution.py:255
  178.4 33.3 %collective-permute-start.75 = (bf16[512,512]{1,0:T(8,128)(2,1)S(1)}, bf16[512,512]{1,0:T(8,128)(2,1)}, u32[]{:S(2)}, u32[]{:S(2)}) collective-permute-start(bf16[512,512]{1,0:T(8,128)(2,1)S(1)} %get-tuple-element.737), channel_id=1, source_target_pairs={{0,8},{16,24},{1,9},{17,25},{2,10},{18,26},{3,11},{19,27},{4,12},{... | collective-permute-start | bytes 1572872 | tf_op jit(solution)/shard_map/ppermute | solution.py:255
  182.2 29.5 %collective-permute-start.73 = (bf16[512,512]{1,0:T(8,128)(2,1)S(1)}, bf16[512,512]{1,0:T(8,128)(2,1)S(1)}, u32[]{:S(2)}, u32[]{:S(2)}) collective-permute-start(bf16[512,512]{1,0:T(8,128)(2,1)S(1)} %get-tuple-element.736), channel_id=1, source_target_pairs={{0,8},{16,24},{1,9},{17,25},{2,10},{18,26},{3,11},{19,27},{4,12},{... | collective-permute-start | bytes 1572872 | tf_op jit(solution)/shard_map/ppermute | solution.py:255
  184.6 61.1 %collective-permute-start.62 = (bf16[192,1792]{1,0:T(8,128)(2,1)S(1)}, bf16[192,1792]{1,0:T(8,128)(2,1)}, u32[]{:S(2)}, u32[]{:S(2)}) collective-permute-start(bf16[192,1792]{1,0:T(8,128)(2,1)S(1)} %slice.343), channel_id=1, source_target_pairs={{0,2},{1,3},{8,10},{9,11},{16,18},{17,19},{24,26},{25,27}} | collective-permute-start | bytes 2064392 | tf_op jit(solution)/shard_map/ppermute | solution.py:311
  209.9 41.7 %collective-permute-start.65 = (bf16[192,1920]{1,0:T(8,128)(2,1)}, bf16[192,1920]{1,0:T(8,128)(2,1)S(1)}, u32[]{:S(2)}, u32[]{:S(2)}) collective-permute-start(bf16[192,1920]{1,0:T(8,128)(2,1)} %slice.349), channel_id=1, source_target_pairs={{0,4},{2,6},{8,12},{10,14},{16,20},{18,22},{24,28},{26,30}} | collective-permute-start | bytes 2211848 | tf_op jit(solution)/shard_map/ppermute | solution.py:311
  210.7 40.0 %collective-permute-start.69 = (bf16[384,1920]{1,0:T(8,128)(2,1)S(1)}, bf16[384,1920]{1,0:T(8,128)(2,1)S(1)}, u32[]{:S(2)}, u32[]{:S(2)}) collective-permute-start(bf16[384,1920]{1,0:T(8,128)(2,1)S(1)} %slice.353), channel_id=1, source_target_pairs={{0,4},{8,12},{16,20},{24,28}} | collective-permute-start | bytes 4423688 | tf_op jit(solution)/shard_map/ppermute | solution.py:311
  247.0 8.4 %collective-permute-start.63 = (bf16[96,1792]{1,0:T(8,128)(2,1)S(1)}, bf16[96,1792]{1,0:T(8,128)(2,1)S(1)}, u32[]{:S(2)}, u32[]{:S(2)}) collective-permute-start(bf16[96,1792]{1,0:T(8,128)(2,1)S(1)} %slice.345), channel_id=1, source_target_pairs={{0,4},{1,5},{2,6},{3,7},{8,12},{9,13},{10,14},{11,15},{16,20},{17,... | collective-permute-start | bytes 1032200 | tf_op jit(solution)/shard_map/ppermute | solution.py:311
  250.9 5.3 %collective-permute-start.70 = (bf16[192,1920]{1,0:T(8,128)(2,1)S(1)}, bf16[192,1920]{1,0:T(8,128)(2,1)S(1)}, u32[]{:S(2)}, u32[]{:S(2)}) collective-permute-start(bf16[192,1920]{1,0:T(8,128)(2,1)S(1)} %slice.355), channel_id=1, source_target_pairs={{0,1},{4,5},{8,9},{12,13},{16,17},{20,21},{24,25},{28,29}} | collective-permute-start | bytes 2211848 | tf_op jit(solution)/shard_map/ppermute | solution.py:311
  251.8 9.4 %collective-permute-start.66 = (bf16[96,1920]{1,0:T(8,128)(2,1)S(1)}, bf16[96,1920]{1,0:T(8,128)(2,1)S(1)}, u32[]{:S(2)}, u32[]{:S(2)}) collective-permute-start(bf16[96,1920]{1,0:T(8,128)(2,1)S(1)} %slice.351), channel_id=1, source_target_pairs={{0,1},{2,3},{4,5},{6,7},{8,9},{10,11},{12,13},{14,15},{16,17},{18,... | collective-permute-start | bytes 1105928 | tf_op jit(solution)/shard_map/ppermute | solution.py:311
  256.3 18.4 %collective-permute-start.71 = (bf16[96,1920]{1,0:T(8,128)(2,1)S(1)}, bf16[96,1920]{1,0:T(8,128)(2,1)S(1)}, u32[]{:S(2)}, u32[]{:S(2)}) collective-permute-start(bf16[96,1920]{1,0:T(8,128)(2,1)S(1)} %slice.357), channel_id=1, source_target_pairs={{0,2},{4,6},{1,3},{5,7},{8,10},{12,14},{9,11},{13,15},{16,18},{20,... | collective-permute-start | bytes 1105928 | tf_op jit(solution)/shard_map/ppermute | solution.py:311
  (34 other events, 320.9 us)
